TPU v7x, 512 devices: a whole 4x4x16 slice. The times are simulated.
512 devices in a mesh: dp: 32 (over z, x_hi), mp: 16 (over x_lo, y, core).
Axes of the slice: x: 4 (x_hi: 2, x_lo: 2; x = x_hi * 2 + x_lo), y: 4, z: 16, core: 2. Of those that a mesh axis runs over, the one named last changes fastest.
Arguments:
- tokens: bfloat16 [32768, 2048], P('dp', 'mp'), may hold values from -6 to 6
- norm_gain: bfloat16 [2048], replicated, may hold values from 0.099609375 to 1.8984375
- wi_gate: bfloat16 [2048, 5120], P(None, 'mp'), may hold values from -0.125 to 0.125
- wi_linear: bfloat16 [2048, 5120], P(None, 'mp'), may hold values from -0.125 to 0.125
- wo_out: bfloat16 [5120, 2048], P('mp'), may hold values from -0.078125 to 0.078125
- task_table: float32 [8, 64], replicated, may hold values from -5 to 5
- layer_table: float32 [24, 64], replicated, may hold values from -5 to 5
- task_ids: int32 [256], P('dp'), may hold values from 0 to 7
- layer_index: int32 [1], replicated, may hold values from 0 to 23
- hyper_in: bfloat16 [128, 1024], P(None, 'mp'), may hold values from -0.5 to 0.5
- gen_down: bfloat16 [1024, 131072], P(None, ('mp', 'dp')), may hold values from -0.0078125 to 0.0078125
- gen_up: bfloat16 [1024, 131072], P(None, ('mp', 'dp')), may hold values from -0.046875 to 0.046875
Outputs:
- mixed: bfloat16 [32768, 2048], P('dp', 'mp')
All inputs are finite; a program needn't handle non-finite values.
Results may differ from a plain program's by a relative error of at most 0.019.
Values may be sent and summed in bfloat16 or wider, within the bound.
No kernel may reach another device: no remote copies, remote signals or barrier semaphores. Data moves between devices by JAX's collectives and lax.ppermute only.
A program may use at most 64 MiB of HBM per device.

v0:
```python
import jax
import jax.numpy as jnp
from jax import lax
from jax.sharding import PartitionSpec as P

R = 64


def laid_out(blocks, dim):
    lengths = list(blocks.shape[1:])
    lengths[dim] *= blocks.shape[0]
    return jnp.moveaxis(blocks, 0, dim).reshape(lengths)


def from_everyone(shard, axis):
    copies = jnp.broadcast_to(shard, (lax.axis_size(axis), *shard.shape))
    return lax.all_to_all(copies, axis, split_axis=0, concat_axis=0, tiled=True)


def gather_directly(shard, axis, dim):
    return laid_out(from_everyone(shard, axis), dim)


def of_everyone(shard, axis):
    everything = from_everyone(shard, axis)
    return jnp.sum(everything.astype(jnp.float32), axis=0)


def matmul(left, right):
    return jnp.dot(left, right, preferred_element_type=jnp.float32)


def per_device(
    tokens,
    norm_gain,
    wi_gate,
    wi_linear,
    wo_out,
    task_table,
    layer_table,
    task_ids,
    layer_index,
    hyper_in,
    gen_down,
    gen_up,
):
    task_count = task_table.shape[0]
    layer_row = jnp.take(layer_table, layer_index, axis=0)
    embed = jnp.concatenate(
        [task_table, jnp.broadcast_to(layer_row, (task_count, layer_row.shape[1]))], axis=1
    ).astype(jnp.bfloat16)
    hidden_part = jnp.maximum(matmul(embed, hyper_in), 0.0).astype(jnp.bfloat16)
    hidden = gather_directly(hidden_part, "mp", 1)
    every_id = gather_directly(task_ids, "dp", 0)
    wanted = jnp.take(hidden, every_id, axis=0)
    made = (
        matmul(wanted, gen_down).astype(jnp.bfloat16),
        matmul(wanted, gen_up).astype(jnp.bfloat16),
    )
    local_down, local_up = (
        lax.all_to_all(made[0], "dp", split_axis=0, concat_axis=1, tiled=True),
        lax.all_to_all(made[1], "dp", split_axis=0, concat_axis=1, tiled=True),
    )
    full_rows = lax.all_gather(tokens, "mp", axis=1, tiled=True)
    wide = full_rows.astype(jnp.float32)
    scale = lax.rsqrt(jnp.mean(wide * wide, axis=-1, keepdims=True) + 1e-06)
    normed = (wide * scale * norm_gain.astype(jnp.float32)).astype(jnp.bfloat16)
    gate = matmul(normed, wi_gate)
    linear = matmul(normed, wi_linear)
    act = (jax.nn.gelu(gate, approximate=True) * linear).astype(jnp.bfloat16)
    seqs_dev = task_ids.shape[0]
    tok_dev = tokens.shape[0]
    seq_len = tok_dev // seqs_dev
    partial_sums = matmul(act, wo_out)
    ffout = lax.psum_scatter(
        partial_sums.astype(jnp.bfloat16), "mp", scatter_dimension=1, tiled=True
    )
    down_block = local_down.reshape(seqs_dev, -1, R)
    up_block = local_up.reshape(seqs_dev, -1, R)
    blocks = ffout.reshape(seqs_dev, seq_len, -1)
    squeeze_part = jnp.einsum(
        "std,sdr->str", blocks, down_block, preferred_element_type=jnp.float32
    )
    squeeze_full = of_everyone(squeeze_part.astype(jnp.bfloat16), "mp").astype(jnp.float32)
    squeezed = jnp.maximum(squeeze_full, 0.0).astype(jnp.bfloat16)
    expand = jnp.einsum("str,sdr->std", squeezed, up_block, preferred_element_type=jnp.float32)
    total = tokens.astype(jnp.float32) + ffout.astype(jnp.float32) + expand.reshape(tok_dev, -1)
    return total.astype(jnp.bfloat16)


def solution(mesh):
    return jax.shard_map(
        per_device,
        mesh=mesh,
        in_specs=(
            P("dp", "mp"),
            P(),
            P(None, "mp"),
            P(None, "mp"),
            P("mp", None),
            P(),
            P(),
            P("dp"),
            P(),
            P(None, "mp"),
            P(None, ("mp", "dp")),
            P(None, ("mp", "dp")),
        ),
        out_specs=P("dp", "mp"),
        check_vma=False,
    )
```

profile of v0, /device:TPU:25, one launch (start us, length us, event | category | flops | bytes accessed | tf_op | source)
XLA Modules:
  0.0 219.2 jit_solution(13709303609028139173)
XLA Ops:
  6.5 0.7 all-gather.2.cloned.1.call-update
  7.3 0.0 reduce-scatter.4.cloned.1.call-start
  7.3 0.7 convert_element_type.45
  8.0 58.1 %all-gather.2.cloned.1.call-done = bf16[1024,2048]{1,0:T(8,128)(2,1)} async-done(((bf16[1024,128]{1,0:T(8,128)(2,1)}), bf16[1024,2048]{1,0:T(8,128)(2,1)}) %all-gather.2.cloned.1.call-update) | async-done | bytes 4194320 | tf_op jit(solution)/shard_map/all_gather | solution.py:64
  66.1 3.2 %fusion = f32[1024]{0:T(1024)S(1)} fusion(bf16[1024,2048]{1,0:T(8,128)(2,1)} %all-gather.2.cloned.1.call-done), kind=kLoop, calls=%fused_computation.3 | loop fusion | flops 6290432 | bytes 4198400 | tf_op jit(solution)/shard_map/reduce_sum | solution.py:66
  69.3 0.2 copy-done.1
  69.5 4.2 %fusion.12 = f32[1024,320]{0,1:T(8,128)} fusion(bf16[2048,320]{0,1:T(8,128)(2,1)} %param.14, bf16[1024,2048]{1,0:T(8,128)(2,1)S(1)} %copy-done.1, f32[2048]{0:T(1024)S(1)} %convert_element_type.45, f32[1024]{0:T(1024)S(1)} %add_rsqrt_fusion), kind=kOutput, calls=%fused_computation.18 | convolution fusion | flops 1350565888 | bytes 6828032 | tf_op jit(solution)/shard_map/dot_general | solution.py:30
  73.8 8.6 %convolution_convert_fusion = bf16[1024,2048]{1,0:T(8,128)(2,1)} fusion(bf16[320,2048]{1,0:T(8,128)(2,1)S(1)} %copy-done, bf16[2048,320]{0,1:T(8,128)(2,1)S(1)} %copy-done.10, f32[1024,320]{0,1:T(8,128)} %fusion.12, bf16[1024,2048]{1,0:T(8,128)(2,1)} %all-gather.2.cloned.1.call-done, f32[2048]{0:T(1024)S(1)} %convert_element_type.45, f32[1024]{0:T(1024)S(1)} %add_rsqrt_fusion), kind=kOutput, calls=%fused_computation.7 | convolution fusion | flops 2698117120 | bytes 12333056 | tf_op jit(solution)/shard_map/dot_general | solution.py:30
  82.4 6.4 %copy.23 = bf16[1024,2048]{0,1:T(8,128)(2,1)} copy(bf16[1024,2048]{1,0:T(8,128)(2,1)} %convolution_convert_fusion) | data formatting | bytes 8388608
  88.8 0.0 reduce-scatter.4.cloned.1.call-update
  88.8 0.6 copy-done.9
  89.4 0.6 broadcast_in_dim.38
  90.0 14.2 %all-to-all-start = ((s32[32,1,8]{2,1,0:T(1,128)}), s32[32,1,8]{2,1,0:T(1,128)S(1)}, u32[]{:S(2)}, u32[]{:S(2)}) async-start(s32[32,1,8]{2,1,0:T(1,128)} %broadcast_in_dim.38), calls=%async_computation | async-start | bytes 32768 | tf_op jit(solution)/shard_map/all_to_all | solution.py:17
  105.0 0.7 fusion.30
  105.7 0.1 pad.3.clone
  105.7 0.1 fusion.18
  105.9 0.7 reshape.145
  106.6 11.3 %all-to-all-done = s32[32,1,8]{2,1,0:T(1,128)S(1)} async-done(((s32[32,1,8]{2,1,0:T(1,128)}), s32[32,1,8]{2,1,0:T(1,128)S(1)}, u32[]{:S(2)}, u32[]{:S(2)}) %all-to-all-start) | async-done | bytes 1056 | tf_op jit(solution)/shard_map/all_to_all | solution.py:17
  117.9 6.1 %all-to-all-start.1 = ((bf16[16,2,256]{2,1,0:T(2,128)(2,1)}), bf16[16,2,256]{2,1,0:T(2,128)(2,1)S(1)}, u32[]{:S(2)}, u32[]{:S(2)}) async-start(bf16[16,2,256]{2,1,0:T(2,128)(2,1)} %reshape.145), calls=%async_computation.1 | async-start | bytes 32768 | tf_op jit(solution)/shard_map/all_to_all | solution.py:17
  124.0 0.1 reshape.91
  124.1 0.6 broadcast.82
  124.7 0.7 reduce.5
  125.4 0.1 reshape.89
  125.6 2.6 %all-to-all-done.1 = bf16[16,2,256]{2,1,0:T(2,128)(2,1)S(1)} async-done(((bf16[16,2,256]{2,1,0:T(2,128)(2,1)}), bf16[16,2,256]{2,1,0:T(2,128)(2,1)S(1)}, u32[]{:S(2)}, u32[]{:S(2)}) %all-to-all-start.1) | async-done | bytes 16416 | tf_op jit(solution)/shard_map/all_to_all | solution.py:17
  128.2 0.1 reshape.146
  128.3 0.1 reshape.90
  128.4 0.0 copy-start.11
  128.4 1.2 gather_fusion
  129.6 0.0 copy-start.12
  129.6 1.0 fusion.14
  130.6 3.8 %all-to-all-start.2 = ((bf16[32,8,256]{2,1,0:T(8,128)(2,1)}), bf16[32,8,256]{2,1,0:T(8,128)(2,1)S(1)}, u32[]{:S(2)}, u32[]{:S(2)}) async-start(bf16[32,8,256]{2,1,0:T(8,128)(2,1)} %fusion.14), calls=%async_computation.2 | async-start | bytes 262144 | tf_op jit(solution)/shard_map/all_to_all | solution.py:61
  134.4 1.0 fusion.15
  135.4 14.6 %all-to-all-done.2 = bf16[32,8,256]{2,1,0:T(8,128)(2,1)S(1)} async-done(((bf16[32,8,256]{2,1,0:T(8,128)(2,1)}), bf16[32,8,256]{2,1,0:T(8,128)(2,1)S(1)}, u32[]{:S(2)}, u32[]{:S(2)}) %all-to-all-start.2) | async-done | bytes 131104 | tf_op jit(solution)/shard_map/all_to_all | solution.py:61
  150.0 5.2 %all-to-all-start.4 = ((bf16[32,8,256]{2,1,0:T(8,128)(2,1)}), bf16[32,8,256]{2,1,0:T(8,128)(2,1)S(1)}, u32[]{:S(2)}, u32[]{:S(2)}) async-start(bf16[32,8,256]{2,1,0:T(8,128)(2,1)} %fusion.15), calls=%async_computation.4 | async-start | bytes 262144 | tf_op jit(solution)/shard_map/all_to_all | solution.py:62
  155.3 0.2 reshape.92
  155.4 7.9 %reduce-scatter.4.cloned.1.call-done = bf16[128,1024]{1,0:T(8,128)(2,1)} async-done(((bf16[2048,1024]{1,0:T(8,128)(2,1)}), bf16[128,1024]{1,0:T(8,128)(2,1)}) %reduce-scatter.4.cloned.1.call-update) | async-done | bytes 262160
  163.4 1.1 copy.24
  164.5 0.3 convolution_convert_fusion.2
  164.8 5.2 %all-to-all-done.4 = bf16[32,8,256]{2,1,0:T(8,128)(2,1)S(1)} async-done(((bf16[32,8,256]{2,1,0:T(8,128)(2,1)}), bf16[32,8,256]{2,1,0:T(8,128)(2,1)S(1)}, u32[]{:S(2)}, u32[]{:S(2)}) %all-to-all-start.4) | async-done | bytes 131104 | tf_op jit(solution)/shard_map/all_to_all | solution.py:62
  170.0 1.9 broadcast_in_dim.46
  171.9 8.9 %all-to-all-start.3 = ((bf16[16,8,128,64]{2,3,1,0:T(8,128)(2,1)}), bf16[16,8,128,64]{2,3,1,0:T(8,128)(2,1)S(1)}, u32[]{:S(2)}, u32[]{:S(2)}) async-start(bf16[16,8,128,64]{2,3,1,0:T(8,128)(2,1)} %broadcast_in_dim.46), calls=%async_computation.3 | async-start | bytes 4194304 | tf_op jit(solution)/shard_map/all_to_all | solution.py:17
  180.8 0.9 copy.19
  181.7 0.9 reshape.93
  182.6 27.8 %all-to-all-done.3 = bf16[16,8,128,64]{2,3,1,0:T(8,128)(2,1)S(1)} async-done(((bf16[16,8,128,64]{2,3,1,0:T(8,128)(2,1)}), bf16[16,8,128,64]{2,3,1,0:T(8,128)(2,1)S(1)}, u32[]{:S(2)}, u32[]{:S(2)}) %all-to-all-start.3) | async-done | bytes 2097184 | tf_op jit(solution)/shard_map/all_to_all | solution.py:17
  210.3 0.3 convert_reduce_fusion
  210.7 0.6 copy-done.5
  211.3 0.3 fusion.24
  211.6 0.8 fusion.23
  (30 shorter events, 0.1 us)
Async XLA Ops:
  6.5 67.2 %copy-start = (bf16[320,2048]{1,0:T(8,128)(2,1)S(1)}, bf16[320,2048]{1,0:T(8,128)(2,1)}, u32[]{:S(2)}) copy-start(bf16[320,2048]{1,0:T(8,128)(2,1)} %param.16) | copy-start | bytes 3932164
  6.5 59.6 %all-gather.2.cloned.1.call-start = ((), (), s32[]{:S(2)}) async-start(), calls=%async_computation.6 | async-start | bytes 4456448 | tf_op jit(solution)/shard_map/all_gather | solution.py:64
  7.3 156.1 %reduce-scatter.4.cloned.1.call-start = ((), (), s32[]{:S(2)}) async-start(), calls=%async_computation.7 | async-start | bytes 4456448
  66.1 3.4 %copy-start.1 = (bf16[1024,2048]{1,0:T(8,128)(2,1)S(1)}, bf16[1024,2048]{1,0:T(8,128)(2,1)}, u32[]{:S(2)}) copy-start(bf16[1024,2048]{1,0:T(8,128)(2,1)} %all-gather.2.cloned.1.call-done) | copy-start | bytes 12582916
  69.5 4.2 %copy-start.10 = (bf16[2048,320]{0,1:T(8,128)(2,1)S(1)}, bf16[2048,320]{0,1:T(8,128)(2,1)}, u32[]{:S(2)}) copy-start(bf16[2048,320]{0,1:T(8,128)(2,1)} %param.15) | copy-start | bytes 3932164
  88.8 0.7 copy-start.9
  88.8 16.2 %copy-start.8 = (f32[8,64]{1,0:T(8,128)S(1)}, f32[8,64]{1,0:T(8,128)}, u32[]{:S(2)}) copy-start(f32[8,64]{1,0:T(8,128)} %param.17) | copy-start | bytes 6148
  88.8 17.0 %copy-start.7 = (bf16[128,64]{0,1:T(8,128)(2,1)S(1)}, bf16[128,64]{0,1:T(8,128)(2,1)}, u32[]{:S(2)}) copy-start(bf16[128,64]{0,1:T(8,128)(2,1)} %param.21) | copy-start | bytes 49156
  90.0 27.9 %all-to-all-start = ((s32[32,1,8]{2,1,0:T(1,128)}), s32[32,1,8]{2,1,0:T(1,128)S(1)}, u32[]{:S(2)}, u32[]{:S(2)}) async-start(s32[32,1,8]{2,1,0:T(1,128)} %broadcast_in_dim.38), calls=%async_computation | async-start | bytes 32768 | tf_op jit(solution)/shard_map/all_to_all | solution.py:17
  117.9 10.2 %all-to-all-start.1 = ((bf16[16,2,256]{2,1,0:T(2,128)(2,1)}), bf16[16,2,256]{2,1,0:T(2,128)(2,1)S(1)}, u32[]{:S(2)}, u32[]{:S(2)}) async-start(bf16[16,2,256]{2,1,0:T(2,128)(2,1)} %reshape.145), calls=%async_computation.1 | async-start | bytes 32768 | tf_op jit(solution)/shard_map/all_to_all | solution.py:17
  128.4 1.2 copy-start.11
  129.6 4.9 %copy-start.12 = (bf16[1024,256]{1,0:T(8,128)(2,1)S(1)}, bf16[1024,256]{1,0:T(8,128)(2,1)}, u32[]{:S(2)}) copy-start(bf16[1024,256]{1,0:T(8,128)(2,1)} %param.23) | copy-start | bytes 1572868
  130.6 19.4 %all-to-all-start.2 = ((bf16[32,8,256]{2,1,0:T(8,128)(2,1)}), bf16[32,8,256]{2,1,0:T(8,128)(2,1)S(1)}, u32[]{:S(2)}, u32[]{:S(2)}) async-start(bf16[32,8,256]{2,1,0:T(8,128)(2,1)} %fusion.14), calls=%async_computation.2 | async-start | bytes 262144 | tf_op jit(solution)/shard_map/all_to_all | solution.py:61
  150.0 20.0 %all-to-all-start.4 = ((bf16[32,8,256]{2,1,0:T(8,128)(2,1)}), bf16[32,8,256]{2,1,0:T(8,128)(2,1)S(1)}, u32[]{:S(2)}, u32[]{:S(2)}) async-start(bf16[32,8,256]{2,1,0:T(8,128)(2,1)} %fusion.15), calls=%async_computation.4 | async-start | bytes 262144 | tf_op jit(solution)/shard_map/all_to_all | solution.py:62
  164.5 7.4 %copy-start.2 = (bf16[1024,128]{1,0:T(8,128)(2,1)}, bf16[1024,128]{1,0:T(8,128)(2,1)S(1)}, u32[]{:S(2)}) copy-start(bf16[1024,128]{1,0:T(8,128)(2,1)S(1)} %copy.24) | copy-start | bytes 786436
  170.0 1.9 copy-start.6
  171.9 38.4 %all-to-all-start.3 = ((bf16[16,8,128,64]{2,3,1,0:T(8,128)(2,1)}), bf16[16,8,128,64]{2,3,1,0:T(8,128)(2,1)S(1)}, u32[]{:S(2)}, u32[]{:S(2)}) async-start(bf16[16,8,128,64]{2,3,1,0:T(8,128)(2,1)} %broadcast_in_dim.46), calls=%async_computation.3 | async-start | bytes 4194304 | tf_op jit(solution)/shard_map/all_to_all | solution.py:17
  210.3 1.0 copy-start.5
  210.3 1.3 copy-start.3
  210.3 1.3 copy-start.4
Sparse Core Ops, SparseCore 0:
  9.4 56.6 all-gather.1
  88.9 74.3 reduce-scatter.3
where the time goes:
time: 220 us; the launch traced here: 219 us
  waiting for transfers between devices  128 us (58%)
  starting transfers between devices  38.3 us (17%)
  local copies, waits for them, and re-layouts  16.4 us (7%)
  matrix products  15.6 us (7%)
  between operations  14.2 us (6%)
  other arithmetic  6.5 us (3%)
    all_gather x1, waiting for transfers between devices, per_device(): full_rows = lax.all_gather(tokens, 'mp', axis=1, tiled=True)  58.1 us
    all_to_all x3, waiting for transfers between devices, from_everyone(): return lax.all_to_all(copies, axis, split_axis=0, concat_axis=0, tiled=True)  41.7 us
    all_to_all x3, starting transfers between devices, from_everyone(): return lax.all_to_all(copies, axis, split_axis=0, concat_axis=0, tiled=True)  29.2 us
    dot_general x5, matrix products, matmul(): return jnp.dot(left, right, preferred_element_type=jnp.float32)  15 us
    all_to_all x1, waiting for transfers between devices, per_device(): lax.all_to_all(made[0], 'dp', split_axis=0, concat_axis=1, tiled=True)  14.6 us
    unnamed x30, local copies, waits for them, and re-layouts  9.83 us
    unnamed x3, waiting for transfers between devices  8.67 us
    all_to_all x1, starting transfers between devices, per_device(): lax.all_to_all(made[1], 'dp', split_axis=0, concat_axis=1, tiled=True)  5.21 us
  transfers between devices with their start and end apart: 7, of which 7 were waited for; matrix products, arithmetic and copies ran while one was open for 5% of the time, Pallas kernels for 0%

commit v1 on v0

--- a/solution.py
+++ b/solution.py
@@ -59,7 +59,10 @@
     )
     local_down, local_up = (
         lax.all_to_all(made[0], "dp", split_axis=0, concat_axis=1, tiled=True),
-        lax.all_to_all(made[1], "dp", split_axis=0, concat_axis=1, tiled=True),
+        jnp.concatenate(
+            lax.all_to_all(jnp.stack(jnp.split(made[1], lax.axis_size("dp"), axis=0)), "dp", 0, 0),
+            axis=1,
+        ),
     )
     full_rows = lax.all_gather(tokens, "mp", axis=1, tiled=True)
     wide = full_rows.astype(jnp.float32)

time: 220 us -> 213 us (0.968)
  waiting for transfers between devices: 128 us -> 81.4 us
  starting transfers between devices: 38.3 us -> 58.5 us
  local copies, waits for them, and re-layouts: 16.4 us -> 35.3 us
    all_gather x1, waiting for transfers between devices: 58.1 us -> 18.8 us  [per_device(): full_rows = lax.all_gather(tokens, 'mp', axis=1, tiled=True)]
    unnamed x30 -> x55, local copies, waits for them, and re-layouts: 9.83 us -> 27.6 us
    unnamed x3, waiting for transfers between devices: 8.67 us -> 25.6 us
    all_to_all x1, waiting for transfers between devices: 14.6 us -> 0.01 us  [per_device(): lax.all_to_all(made[0], 'dp', split_axis=0, concat_axis=1, tiled=True)]
    all_to_all x1, starting transfers between devices: 3.84 us -> 14.2 us  [per_device(): lax.all_to_all(made[0], 'dp', split_axis=0, concat_axis=1, tiled=True)]
    all_to_all x1, starting transfers between devices: 5.21 us -> 14 us  [per_device(): lax.all_to_all(jnp.stack(jnp.split(made[1], lax.axis_size('dp'), axis=0))...]
    all_to_all x1, waiting for transfers between devices: 5.21 us -> 0.02 us  [per_device(): lax.all_to_all(jnp.stack(jnp.split(made[1], lax.axis_size('dp'), axis=0))...]
    all_to_all x3, waiting for transfers between devices: 41.7 us -> 37 us  [from_everyone(): return lax.all_to_all(copies, axis, split_axis=0, concat_axis=0, tiled=True)]
  transfers between devices with their start and end apart: 7 -> 7, of which waited for: 7 -> 4; matrix products, arithmetic and copies ran while one was open for 5% -> 25% of each run, Pallas kernels for 0% -> 0%
where the time goes in v1:
time: 213 us; the launch traced here: 212 us
  waiting for transfers between devices  81.4 us (38%)
  starting transfers between devices  58.5 us (27%)
  local copies, waits for them, and re-layouts  35.3 us (17%)
  matrix products  15.6 us (7%)
  between operations  14.3 us (7%)
  other arithmetic  7.06 us (3%)
    all_to_all x3, waiting for transfers between devices, from_everyone(): return lax.all_to_all(copies, axis, split_axis=0, concat_axis=0, tiled=True)  37 us
    all_to_all x3, starting transfers between devices, from_everyone(): return lax.all_to_all(copies, axis, split_axis=0, concat_axis=0, tiled=True)  30.2 us
    unnamed x55, local copies, waits for them, and re-layouts  27.6 us
    unnamed x3, waiting for transfers between devices  25.6 us
    all_gather x1, waiting for transfers between devices, per_device(): full_rows = lax.all_gather(tokens, 'mp', axis=1, tiled=True)  18.8 us
    dot_general x5, matrix products, matmul(): return jnp.dot(left, right, preferred_element_type=jnp.float32)  15 us
    all_to_all x1, starting transfers between devices, per_device(): lax.all_to_all(made[0], 'dp', split_axis=0, concat_axis=1, tiled=True)  14.2 us
    all_to_all x1, starting transfers between devices, per_device(): lax.all_to_all(jnp.stack(jnp.split(made[1], lax.axis_size('dp'), axis=0))...  14 us
  transfers between devices with their start and end apart: 7, of which 4 were waited for; matrix products, arithmetic and copies ran while one was open for 25% of the time, Pallas kernels for 0%

profile of v1, /device:TPU:25, one launch (start us, length us, event | category | flops | bytes accessed | tf_op | source)
XLA Modules:
  0.0 212.1 jit_solution(1439686125442147526)
XLA Ops:
  6.5 0.7 all-gather.2.cloned.1.call-update
  7.3 1.3 broadcast_in_dim.38
  8.5 17.7 %all-to-all-start = ((s32[32,1,8]{2,1,0:T(1,128)}), s32[32,1,8]{2,1,0:T(1,128)S(1)}, u32[]{:S(2)}, u32[]{:S(2)}) async-start(s32[32,1,8]{2,1,0:T(1,128)} %broadcast_in_dim.38), calls=%async_computation | async-start | bytes 32768 | tf_op jit(solution)/shard_map/all_to_all | solution.py:17
  26.8 0.7 convert.7
  27.5 0.7 fusion.29
  28.3 0.8 fusion.17
  29.2 0.7 convert_element_type.45
  29.9 0.7 reshape.141
  30.6 9.2 %all-to-all-done = s32[32,1,8]{2,1,0:T(1,128)S(1)} async-done(((s32[32,1,8]{2,1,0:T(1,128)}), s32[32,1,8]{2,1,0:T(1,128)S(1)}, u32[]{:S(2)}, u32[]{:S(2)}) %all-to-all-start) | async-done | bytes 1056 | tf_op jit(solution)/shard_map/all_to_all | solution.py:17
  39.8 6.4 %all-to-all-start.1 = ((bf16[16,2,256]{2,1,0:T(2,128)(2,1)}), bf16[16,2,256]{2,1,0:T(2,128)(2,1)S(1)}, u32[]{:S(2)}, u32[]{:S(2)}) async-start(bf16[16,2,256]{2,1,0:T(2,128)(2,1)} %reshape.141), calls=%async_computation.1 | async-start | bytes 32768 | tf_op jit(solution)/shard_map/all_to_all | solution.py:17
  47.5 18.8 %all-gather.2.cloned.1.call-done = bf16[1024,2048]{1,0:T(8,128)(2,1)} async-done(((bf16[1024,128]{1,0:T(8,128)(2,1)}), bf16[1024,2048]{1,0:T(8,128)(2,1)}) %all-gather.2.cloned.1.call-update) | async-done | bytes 4194320 | tf_op jit(solution)/shard_map/all_gather | solution.py:67
  66.3 3.2 %fusion = f32[1024]{0:T(1024)S(1)} fusion(bf16[1024,2048]{1,0:T(8,128)(2,1)} %all-gather.2.cloned.1.call-done), kind=kLoop, calls=%fused_computation.3 | loop fusion | flops 6290432 | bytes 4198400 | tf_op jit(solution)/shard_map/reduce_sum | solution.py:69
  69.8 4.2 %fusion.12 = f32[1024,320]{0,1:T(8,128)} fusion(bf16[2048,320]{0,1:T(8,128)(2,1)} %param.14, bf16[1024,2048]{1,0:T(8,128)(2,1)S(1)} %copy-done.1, f32[2048]{0:T(1024)S(1)} %convert_element_type.45, f32[1024]{0:T(1024)S(1)} %add_rsqrt_fusion), kind=kOutput, calls=%fused_computation.18 | convolution fusion | flops 1350565888 | bytes 6828032 | tf_op jit(solution)/shard_map/dot_general | solution.py:30
  74.0 8.6 %convolution_convert_fusion = bf16[1024,2048]{1,0:T(8,128)(2,1)} fusion(bf16[320,2048]{1,0:T(8,128)(2,1)S(1)} %copy-done, bf16[2048,320]{0,1:T(8,128)(2,1)S(1)} %copy-done.7, f32[1024,320]{0,1:T(8,128)} %fusion.12, bf16[1024,2048]{1,0:T(8,128)(2,1)} %all-gather.2.cloned.1.call-done, f32[2048]{0:T(1024)S(1)} %convert_element_type.45, f32[1024]{0:T(1024)S(1)} %add_rsqrt_fusion), kind=kOutput, calls=%fused_computation.7 | convolution fusion | flops 2698117120 | bytes 12333056 | tf_op jit(solution)/shard_map/dot_general | solution.py:30
  82.6 6.4 %copy.23 = bf16[1024,2048]{0,1:T(8,128)(2,1)} copy(bf16[1024,2048]{1,0:T(8,128)(2,1)} %convolution_convert_fusion) | data formatting | bytes 8388608
  89.3 1.2 gather_fusion
  90.5 1.0 fusion.14
  91.5 14.2 %all-to-all-start.2 = ((bf16[32,8,256]{2,1,0:T(8,128)(2,1)}), bf16[32,8,256]{2,1,0:T(8,128)(2,1)S(1)}, u32[]{:S(2)}, u32[]{:S(2)}) async-start(bf16[32,8,256]{2,1,0:T(8,128)(2,1)} %fusion.14), calls=%async_computation.2 | async-start | bytes 262144 | tf_op jit(solution)/shard_map/all_to_all | solution.py:61
  106.0 0.6 constant_dynamic-update-slice_fusion.31
  106.6 0.6 constant_dynamic-update-slice_fusion.30
  107.8 0.6 constant_dynamic-update-slice_fusion.28
  108.4 0.6 constant_dynamic-update-slice_fusion.27
  109.0 0.6 constant_dynamic-update-slice_fusion.26
  109.6 0.6 constant_dynamic-update-slice_fusion.25
  110.8 0.6 constant_dynamic-update-slice_fusion.23
  111.4 0.6 constant_dynamic-update-slice_fusion.22
  112.0 0.6 constant_dynamic-update-slice_fusion.21
  112.6 0.6 constant_dynamic-update-slice_fusion.20
  113.2 0.6 constant_dynamic-update-slice_fusion.19
  113.8 0.6 constant_dynamic-update-slice_fusion.18
  114.3 0.6 constant_dynamic-update-slice_fusion.17
  114.9 0.6 constant_dynamic-update-slice_fusion.16
  115.5 0.6 constant_dynamic-update-slice_fusion.15
  116.1 0.6 constant_dynamic-update-slice_fusion.14
  116.7 0.6 constant_dynamic-update-slice_fusion.13
  117.3 0.6 constant_dynamic-update-slice_fusion.12
  117.9 0.6 constant_dynamic-update-slice_fusion.11
  119.1 0.6 constant_dynamic-update-slice_fusion.9
  125.0 14.0 %all-to-all-start.4 = ((bf16[32,8,256]{2,1,0:T(8,128)(2,1)}), bf16[32,8,256]{2,1,0:T(8,128)(2,1)S(1)}, u32[]{:S(2)}, u32[]{:S(2)}) async-start(bf16[32,8,256]{2,1,0:T(8,128)(2,1)} %constant_dynamic-update-slice_fusion), calls=%async_computation.4 | async-start | bytes 262144 | tf_op jit(solution)/shard_map/all_to_all | solution.py:63
  139.3 24.9 %reduce-scatter.4.cloned.1.call-done = bf16[128,1024]{1,0:T(8,128)(2,1)} async-done(((bf16[2048,1024]{1,0:T(8,128)(2,1)}), bf16[128,1024]{1,0:T(8,128)(2,1)}) %reduce-scatter.4.cloned.1.call-update) | async-done | bytes 262160
  164.2 1.1 copy.24
  165.6 1.9 broadcast_in_dim.46
  167.5 6.1 %all-to-all-start.3 = ((bf16[16,8,128,64]{2,3,1,0:T(8,128)(2,1)}), bf16[16,8,128,64]{2,3,1,0:T(8,128)(2,1)S(1)}, u32[]{:S(2)}, u32[]{:S(2)}) async-start(bf16[16,8,128,64]{2,3,1,0:T(8,128)(2,1)} %broadcast_in_dim.46), calls=%async_computation.3 | async-start | bytes 4194304 | tf_op jit(solution)/shard_map/all_to_all | solution.py:17
  173.6 0.9 copy.19
  174.5 0.9 reshape_reshape.3
  175.4 27.8 %all-to-all-done.3 = bf16[16,8,128,64]{2,3,1,0:T(8,128)(2,1)S(1)} async-done(((bf16[16,8,128,64]{2,3,1,0:T(8,128)(2,1)}), bf16[16,8,128,64]{2,3,1,0:T(8,128)(2,1)S(1)}, u32[]{:S(2)}, u32[]{:S(2)}) %all-to-all-start.3) | async-done | bytes 2097184 | tf_op jit(solution)/shard_map/all_to_all | solution.py:17
  203.5 0.6 copy-done.5
  204.4 0.8 fusion.22
  (56 shorter events, 10.5 us)
Async XLA Ops:
  6.5 67.4 %copy-start = (bf16[320,2048]{1,0:T(8,128)(2,1)S(1)}, bf16[320,2048]{1,0:T(8,128)(2,1)}, u32[]{:S(2)}) copy-start(bf16[320,2048]{1,0:T(8,128)(2,1)} %param.16) | copy-start | bytes 3932164
  6.5 59.8 %all-gather.2.cloned.1.call-start = ((), (), s32[]{:S(2)}) async-start(), calls=%async_computation.6 | async-start | bytes 4456448 | tf_op jit(solution)/shard_map/all_gather | solution.py:67
  8.5 31.2 %all-to-all-start = ((s32[32,1,8]{2,1,0:T(1,128)}), s32[32,1,8]{2,1,0:T(1,128)S(1)}, u32[]{:S(2)}, u32[]{:S(2)}) async-start(s32[32,1,8]{2,1,0:T(1,128)} %broadcast_in_dim.38), calls=%async_computation | async-start | bytes 32768 | tf_op jit(solution)/shard_map/all_to_all | solution.py:17
  39.8 49.3 %all-to-all-start.1 = ((bf16[16,2,256]{2,1,0:T(2,128)(2,1)}), bf16[16,2,256]{2,1,0:T(2,128)(2,1)S(1)}, u32[]{:S(2)}, u32[]{:S(2)}) async-start(bf16[16,2,256]{2,1,0:T(2,128)(2,1)} %reshape.141), calls=%async_computation.1 | async-start | bytes 32768 | tf_op jit(solution)/shard_map/all_to_all | solution.py:17
  46.2 117.9 %reduce-scatter.4.cloned.1.call-start = ((), (), s32[]{:S(2)}) async-start(), calls=%async_computation.7 | async-start | bytes 4456448
  66.3 3.4 %copy-start.1 = (bf16[1024,2048]{1,0:T(8,128)(2,1)S(1)}, bf16[1024,2048]{1,0:T(8,128)(2,1)}, u32[]{:S(2)}) copy-start(bf16[1024,2048]{1,0:T(8,128)(2,1)} %all-gather.2.cloned.1.call-done) | copy-start | bytes 12582916
  69.8 4.2 %copy-start.7 = (bf16[2048,320]{0,1:T(8,128)(2,1)S(1)}, bf16[2048,320]{0,1:T(8,128)(2,1)}, u32[]{:S(2)}) copy-start(bf16[2048,320]{0,1:T(8,128)(2,1)} %param.15) | copy-start | bytes 3932164
  89.3 1.2 copy-start.8
  90.5 15.2 %copy-start.9 = (bf16[1024,256]{1,0:T(8,128)(2,1)S(1)}, bf16[1024,256]{1,0:T(8,128)(2,1)}, u32[]{:S(2)}) copy-start(bf16[1024,256]{1,0:T(8,128)(2,1)} %param.23) | copy-start | bytes 1572868
  91.5 33.6 %all-to-all-start.2 = ((bf16[32,8,256]{2,1,0:T(8,128)(2,1)}), bf16[32,8,256]{2,1,0:T(8,128)(2,1)S(1)}, u32[]{:S(2)}, u32[]{:S(2)}) async-start(bf16[32,8,256]{2,1,0:T(8,128)(2,1)} %fusion.14), calls=%async_computation.2 | async-start | bytes 262144 | tf_op jit(solution)/shard_map/all_to_all | solution.py:61
  125.0 40.6 %all-to-all-start.4 = ((bf16[32,8,256]{2,1,0:T(8,128)(2,1)}), bf16[32,8,256]{2,1,0:T(8,128)(2,1)S(1)}, u32[]{:S(2)}, u32[]{:S(2)}) async-start(bf16[32,8,256]{2,1,0:T(8,128)(2,1)} %constant_dynamic-update-slice_fusion), calls=%async_computation.4 | async-start | bytes 262144 | tf_op jit(solution)/shard_map/all_to_all | solution.py:63
  165.3 2.2 %copy-start.2 = (bf16[1024,128]{1,0:T(8,128)(2,1)}, bf16[1024,128]{1,0:T(8,128)(2,1)S(1)}, u32[]{:S(2)}) copy-start(bf16[1024,128]{1,0:T(8,128)(2,1)S(1)} %copy.24) | copy-start | bytes 786436
  165.6 1.9 copy-start.6
  167.5 35.7 %all-to-all-start.3 = ((bf16[16,8,128,64]{2,3,1,0:T(8,128)(2,1)}), bf16[16,8,128,64]{2,3,1,0:T(8,128)(2,1)S(1)}, u32[]{:S(2)}, u32[]{:S(2)}) async-start(bf16[16,8,128,64]{2,3,1,0:T(8,128)(2,1)} %broadcast_in_dim.46), calls=%async_computation.3 | async-start | bytes 4194304 | tf_op jit(solution)/shard_map/all_to_all | solution.py:17
  203.2 1.0 copy-start.5
  203.2 1.3 copy-start.3
  203.2 1.3 copy-start.4
Sparse Core Ops, SparseCore 0:
  9.4 56.8 all-gather.1
  89.1 74.9 reduce-scatter.3
